TPU v7x, 32 devices: a whole 2x2x4 slice. The times are simulated.
32 devices in a mesh: seq: 8 (over y, x, core), fsdp: 4 (over z).
Axes of the slice: x: 2, y: 2, z: 4, core: 2. Of those that a mesh axis runs over, the one named last changes fastest.
Arguments:
- normed: bfloat16 [32768, 1024], P(('seq', 'fsdp')), may hold values from -31 to 31, as said below
- w_qkv: bfloat16 [1024, 3072], P('fsdp'), may hold values from -0.5 to 0.5, as said below
- w_out: bfloat16 [1024, 1024], P('fsdp'), may hold values from -0.5 to 0.5
- layout: int32 [256, 10], P(('seq', 'fsdp')), may hold values from 0 to 23, as said below
- counts: int32 [256], P(('seq', 'fsdp')), may hold values from 1 to 10, as said below
Outputs:
- mixed: bfloat16 [32768, 1024], P(('seq', 'fsdp'))
Inputs may be any that keep to these rules, and one draw needn't show every extreme that they name: `normed`: float activations. `w_qkv`: float weights. `layout`: each row holds 10 distinct pool entries, never the query block's own entry; entries 0 to 7 name the blocks of the station one step lower along seq, the last 8 those one step higher. `counts`: the value 10 occurs in every draw.
All inputs are finite; a program needn't handle non-finite values.
Results may differ from a plain program's by a relative error of at most 0.0099.
Values may be sent and summed in bfloat16 or wider, within the bound.
No kernel may reach another device: no remote copies, remote signals or barrier semaphores. Data moves between devices by JAX's collectives and lax.ppermute only.
A program may use at most 128 MiB of HBM per device.

v0:
```python
import math
import jax
import jax.numpy as jnp
from jax import lax
from jax.sharding import PartitionSpec as P

HEADS = 8
BLOCK = 128
KEY_BLOCKS = 10


def from_behind(value, axis, steps):
    count = lax.axis_size(axis)
    pairs = [(source, (source + steps) % count) for source in range(count)]
    return lax.ppermute(value, axis, pairs)


def attend(query, own_blocks, picked, used):
    block_count = picked.shape[0]
    feature_width = query.shape[1]
    head_width = feature_width // HEADS
    keyvals = jnp.concatenate([own_blocks[:, None], picked], axis=1)
    keyvals = keyvals.reshape(block_count, (KEY_BLOCKS + 1) * BLOCK, 2 * feature_width)
    key_heads = keyvals[..., :feature_width].reshape(block_count, -1, HEADS, head_width)
    value_heads = keyvals[..., feature_width:].reshape(block_count, -1, HEADS, head_width)
    query_heads = query.reshape(block_count, BLOCK, HEADS, head_width)
    scores = jnp.einsum(
        "bqhd,bkhd->bhqk", query_heads, key_heads, preferred_element_type=jnp.float32
    )
    scores = scores * head_width ** (-0.5)
    slot_number = jnp.arange((KEY_BLOCKS + 1) * BLOCK, dtype=jnp.int32) // BLOCK
    usable = slot_number[None, :] <= used[:, None]
    scores = jnp.where(usable[:, None, None, :], scores, -jnp.inf)
    largest = jnp.max(scores, axis=-1, keepdims=True)
    expons = jnp.exp(scores - largest)
    denominator = jnp.sum(expons, axis=-1, keepdims=True)
    rounded = expons.astype(jnp.bfloat16)
    summed = jnp.einsum("bhqk,bkhd->bqhd", rounded, value_heads, preferred_element_type=jnp.float32)
    summed = summed / jnp.transpose(denominator, (0, 2, 1, 3))
    return summed.reshape(block_count * BLOCK, feature_width).astype(jnp.bfloat16)


def shards(normed, w_qkv, w_out, layout, counts):
    row_count, feature_width = normed.shape
    blocks_here = row_count // BLOCK
    lower_tokens = from_behind(normed, "seq", 1)
    upper_tokens = from_behind(normed, "seq", -1)
    sources = (normed, lower_tokens, upper_tokens)
    start_sums = [jnp.zeros((row_count, 3 * feature_width), jnp.float32)]
    for member in range(1, len(sources)):
        start_sums.append(jnp.zeros((row_count, 2 * feature_width), jnp.float32))
    start_sums = tuple(start_sums)
    weight_rows = lax.all_gather(w_qkv, "fsdp", axis=0, tiled=True)
    own_cols = sources[0]
    fresh = [jnp.dot(own_cols, weight_rows, preferred_element_type=jnp.float32)]
    for member in range(1, len(sources)):
        side_cols = sources[member]
        fresh.append(
            jnp.dot(side_cols, weight_rows[:, feature_width:], preferred_element_type=jnp.float32)
        )
    sums = tuple(fresh)
    packed = sums[0].astype(jnp.bfloat16)
    queries = packed[:, :feature_width]
    keyvals = packed[:, feature_width:]
    pool_rows = jnp.concatenate(
        [sums[1].astype(jnp.bfloat16), keyvals, sums[2].astype(jnp.bfloat16)], axis=0
    )
    pool = pool_rows.reshape(3 * blocks_here, BLOCK, 2 * feature_width)
    group_size = math.gcd(blocks_here, max(1, 256 // BLOCK))
    group_count = blocks_here // group_size

    def one_group(items):
        query_part, layout_part, count_part, group_number = items
        own_blocks = lax.dynamic_slice_in_dim(
            pool, blocks_here + group_number * group_size, group_size, 0
        )
        picked = pool[layout_part]
        return attend(query_part, own_blocks, picked, count_part)

    attended = lax.map(
        one_group,
        (
            queries.reshape(group_count, group_size * BLOCK, feature_width),
            layout.reshape(group_count, group_size, KEY_BLOCKS),
            counts.reshape(group_count, group_size),
            jnp.arange(group_count, dtype=jnp.int32),
        ),
    )
    attended = attended.reshape(row_count, feature_width)
    output_sum = jnp.dot(
        attended,
        lax.all_gather(w_out, "fsdp", axis=0, tiled=True),
        preferred_element_type=jnp.float32,
    )
    return output_sum.astype(jnp.bfloat16)


def solution(mesh):
    return jax.shard_map(
        shards,
        mesh=mesh,
        in_specs=(
            P(("seq", "fsdp"), None),
            P("fsdp", None),
            P("fsdp", None),
            P(("seq", "fsdp"), None),
            P(("seq", "fsdp")),
        ),
        out_specs=P(("seq", "fsdp"), None),
        check_vma=False,
    )
```

profile of v0, /device:TPU:0, one launch (start us, length us, event | category | flops | bytes accessed | tf_op | source)
XLA Modules:
  0.0 460.4 jit_solution(16126469676680698676)
XLA Ops:
  6.5 0.7 all-gather.3.cloned.1.call-update
  7.3 3.4 collective-permute-start.1
  10.8 0.7 reshape.143
  11.5 115.5 %all-gather.3.cloned.1.call-done = bf16[1024,3072]{1,0:T(8,128)(2,1)} async-done(((bf16[256,3072]{1,0:T(8,128)(2,1)}), bf16[1024,3072]{1,0:T(8,128)(2,1)}) %all-gather.3.cloned.1.call-update) | async-done | bytes 6291472 | tf_op jit(solution)/shard_map/all_gather | solution.py:53
  127.0 9.4 %convolution_convert_fusion = bf16[1024,3072]{1,0:T(8,128)(2,1)S(1)} fusion(bf16[1024,1024]{1,0:T(8,128)(2,1)} %param.7, bf16[1024,3072]{1,0:T(8,128)(2,1)} %all-gather.3.cloned.1.call-done), kind=kOutput, calls=%fused_computation.36 | convolution fusion | flops 6445596672 | bytes 14680064 | tf_op jit(solution)/shard_map/dot_general | solution.py:55
  136.4 3.2 copy-done.1
  139.6 1.9 copy-done.2
  141.5 6.3 %convolution_convert_fusion.1 = bf16[1024,2048]{1,0:T(8,128)(2,1)S(1)} fusion(bf16[1024,1024]{1,0:T(8,128)(2,1)} %collective-permute-done.1, bf16[1024,3072]{1,0:T(8,128)(2,1)S(1)} %copy-done.2), kind=kOutput, calls=%fused_computation.37 | convolution fusion | flops 4297064448 | bytes 10485760 | tf_op jit(solution)/shard_map/dot_general | solution.py:59
  147.8 4.7 %convolution_convert_fusion.2 = bf16[1024,2048]{1,0:T(8,128)(2,1)S(1)} fusion(bf16[1024,1024]{1,0:T(8,128)(2,1)S(1)} %collective-permute-done, bf16[1024,3072]{1,0:T(8,128)(2,1)S(1)} %copy-done.2), kind=kOutput, calls=%fused_computation.38 | convolution fusion | flops 4297064448 | bytes 10485760 | tf_op jit(solution)/shard_map/dot_general | solution.py:59
  152.6 21.3 %pad_maximum_fusion.1 = bf16[3072,2048]{1,0:T(8,128)(2,1)} fusion(bf16[1024,2048]{1,0:T(8,128)(2,1)S(1)} %convolution_convert_fusion.1, bf16[1024,2048]{1,0:T(8,128)(2,1)S(1)} %slice-done, bf16[1024,2048]{1,0:T(8,128)(2,1)S(1)} %convolution_convert_fusion.2), kind=kLoop, calls=%fused_computation.35 | loop fusion | flops 37748736 | bytes 25165824 | tf_op jit(solution)/shard_map/concatenate | solution.py:65
  173.9 273.7 %while.12 = (s32[]{:T(128)}, bf16[4,256,1024]{2,1,0:T(8,128)(2,1)}, s32[4]{0:T(128)S(1)}, bf16[24,128,2048]{2,1,0:T(8,128)(2,1)}, s32[4,2,10]{2,1,0:T(2,128)}, /...) while((s32[]{:T(128)}, bf16[4,256,1024]{2,1,0:T(8,128)(2,1)}, ...), condition=%wide.region_3.4_spmd, body=%wide.region_0.3_spmd.sunk | while | flops 1514416896 | bytes 190909680 | solution.py:80
  173.9 0.6 dynamic_slice.53
  175.2 1.3 dynamic-slice_bitcast_fusion.4
  176.5 0.7 compare_select_fusion.2
  177.3 10.0 %gather_fusion = bf16[20,128,2048]{2,1,0:T(8,128)(2,1)} fusion(bf16[24,128,2048]{2,1,0:T(8,128)(2,1)} %get-tuple-element.200, s32[1024]{0:T(1024)S(1)} %pad_clamp_fusion.2), kind=kCustom, calls=%fused_computation.clone.1 | custom fusion | bytes 20971600 | tf_op jit(solution)/shard_map/while/body/eval_jaxpr/gather | solution.py:77
  187.3 10.1 %pad_maximum_fusion.3 = bf16[2,11,128,2048]{3,2,1,0:T(8,128)(2,1)} fusion(bf16[2,10,128,2048]{3,2,1,0:T(8,128)(2,1)} %bitcast.76, bf16[2,1,128,2048]{3,2,1,0:T(8,128)(2,1)S(1)} %dynamic-slice_bitcast_fusion.4), kind=kLoop, calls=%fused_computation.1.clone.1 | loop fusion | flops 5767168 | bytes 23068672 | tf_op jit(solution)/shard_map/while/body/eval_jaxpr/concatenate | solution.py:22
  197.3 9.9 %fusion.44 = (bf16[2,1408,1024]{2,1,0:T(8,128)(2,1)}, bf16[2,1408,1024]{2,1,0:T(8,128)(2,1)}) fusion(bf16[2,1408,2048]{2,1,0:T(8,128)(2,1)} %bitcast.74), kind=kLoop, calls=%fused_computation.42.clone.1 | loop fusion | bytes 23068672 | tf_op jit(solution)/shard_map/while/body/eval_jaxpr/slice | solution.py:24
  207.3 8.2 %copy.26 = bf16[2,1408,1024]{1,2,0:T(8,128)(2,1)} copy(bf16[2,1408,1024]{2,1,0:T(8,128)(2,1)} %get-tuple-element.170) | data formatting | bytes 11534336 | tf_op jit(solution)/shard_map/while/body/eval_jaxpr/slice | solution.py:24
  215.7 3.9 fusion.46
  219.6 2.4 fusion.47
  222.1 1.8 copy-done
  223.8 8.3 %copy.25 = bf16[2,1408,1024]{1,2,0:T(8,128)(2,1)} copy(bf16[2,1408,1024]{2,1,0:T(8,128)(2,1)} %get-tuple-element.169) | data formatting | bytes 11534336 | tf_op jit(solution)/shard_map/while/body/eval_jaxpr/slice | solution.py:25
  232.2 8.8 %divide_convert_fusion.2 = bf16[2,128,8,128]{1,3,2,0:T(8,128)(2,1)S(1)} fusion(bf16[2,1408,8,128]{1,3,2,0:T(8,128)(2,1)} %bitcast.78, f32[2,8,128,1408]{3,2,1,0:T(8,128)} %copy-done, f32[2,8,128]{2,1,0:T(8,128)S(1)} %get-tuple-element.172, pred[2,1408]{1,0:T(4,128)(4,1)S(1)} %broadcast_compare_fusion.2, f32[2,128,8]{1,2,0:T(8,128)S(1)} %bitcast.81), kind=kOutput, calls=%fused_computation.13.clone.1 | convolution fusion | flops 750256128 | bytes 17844992 | tf_op jit(solution)/shard_map/while/body/eval_jaxpr/bhqk,bkhd->bqhd/dot_general | solution.py:38
  241.5 0.8 constant_dynamic-update-slice_fusion.2
  242.3 0.6 dynamic_slice.53
  243.6 1.3 dynamic-slice_bitcast_fusion.4
  244.9 0.7 compare_select_fusion.2
  245.7 10.0 %gather_fusion = bf16[20,128,2048]{2,1,0:T(8,128)(2,1)} fusion(bf16[24,128,2048]{2,1,0:T(8,128)(2,1)} %get-tuple-element.200, s32[1024]{0:T(1024)S(1)} %pad_clamp_fusion.2), kind=kCustom, calls=%fused_computation.clone.1 | custom fusion | bytes 20971600 | tf_op jit(solution)/shard_map/while/body/eval_jaxpr/gather | solution.py:77
  255.7 10.1 %pad_maximum_fusion.3 = bf16[2,11,128,2048]{3,2,1,0:T(8,128)(2,1)} fusion(bf16[2,10,128,2048]{3,2,1,0:T(8,128)(2,1)} %bitcast.76, bf16[2,1,128,2048]{3,2,1,0:T(8,128)(2,1)S(1)} %dynamic-slice_bitcast_fusion.4), kind=kLoop, calls=%fused_computation.1.clone.1 | loop fusion | flops 5767168 | bytes 23068672 | tf_op jit(solution)/shard_map/while/body/eval_jaxpr/concatenate | solution.py:22
  265.8 9.9 %fusion.44 = (bf16[2,1408,1024]{2,1,0:T(8,128)(2,1)}, bf16[2,1408,1024]{2,1,0:T(8,128)(2,1)}) fusion(bf16[2,1408,2048]{2,1,0:T(8,128)(2,1)} %bitcast.74), kind=kLoop, calls=%fused_computation.42.clone.1 | loop fusion | bytes 23068672 | tf_op jit(solution)/shard_map/while/body/eval_jaxpr/slice | solution.py:24
  275.7 8.2 %copy.26 = bf16[2,1408,1024]{1,2,0:T(8,128)(2,1)} copy(bf16[2,1408,1024]{2,1,0:T(8,128)(2,1)} %get-tuple-element.170) | data formatting | bytes 11534336 | tf_op jit(solution)/shard_map/while/body/eval_jaxpr/slice | solution.py:24
  284.2 3.9 fusion.46
  288.1 2.4 fusion.47
  290.5 1.8 copy-done
  292.2 8.3 %copy.25 = bf16[2,1408,1024]{1,2,0:T(8,128)(2,1)} copy(bf16[2,1408,1024]{2,1,0:T(8,128)(2,1)} %get-tuple-element.169) | data formatting | bytes 11534336 | tf_op jit(solution)/shard_map/while/body/eval_jaxpr/slice | solution.py:25
  300.6 8.8 %divide_convert_fusion.2 = bf16[2,128,8,128]{1,3,2,0:T(8,128)(2,1)S(1)} fusion(bf16[2,1408,8,128]{1,3,2,0:T(8,128)(2,1)} %bitcast.78, f32[2,8,128,1408]{3,2,1,0:T(8,128)} %copy-done, f32[2,8,128]{2,1,0:T(8,128)S(1)} %get-tuple-element.172, pred[2,1408]{1,0:T(4,128)(4,1)S(1)} %broadcast_compare_fusion.2, f32[2,128,8]{1,2,0:T(8,128)S(1)} %bitcast.81), kind=kOutput, calls=%fused_computation.13.clone.1 | convolution fusion | flops 750256128 | bytes 17844992 | tf_op jit(solution)/shard_map/while/body/eval_jaxpr/bhqk,bkhd->bqhd/dot_general | solution.py:38
  309.9 0.9 constant_dynamic-update-slice_fusion.2
  310.8 0.6 dynamic_slice.53
  312.1 1.3 dynamic-slice_bitcast_fusion.4
  313.4 0.7 compare_select_fusion.2
  314.1 10.0 %gather_fusion = bf16[20,128,2048]{2,1,0:T(8,128)(2,1)} fusion(bf16[24,128,2048]{2,1,0:T(8,128)(2,1)} %get-tuple-element.200, s32[1024]{0:T(1024)S(1)} %pad_clamp_fusion.2), kind=kCustom, calls=%fused_computation.clone.1 | custom fusion | bytes 20971600 | tf_op jit(solution)/shard_map/while/body/eval_jaxpr/gather | solution.py:77
  324.1 10.1 %pad_maximum_fusion.3 = bf16[2,11,128,2048]{3,2,1,0:T(8,128)(2,1)} fusion(bf16[2,10,128,2048]{3,2,1,0:T(8,128)(2,1)} %bitcast.76, bf16[2,1,128,2048]{3,2,1,0:T(8,128)(2,1)S(1)} %dynamic-slice_bitcast_fusion.4), kind=kLoop, calls=%fused_computation.1.clone.1 | loop fusion | flops 5767168 | bytes 23068672 | tf_op jit(solution)/shard_map/while/body/eval_jaxpr/concatenate | solution.py:22
  334.2 9.9 %fusion.44 = (bf16[2,1408,1024]{2,1,0:T(8,128)(2,1)}, bf16[2,1408,1024]{2,1,0:T(8,128)(2,1)}) fusion(bf16[2,1408,2048]{2,1,0:T(8,128)(2,1)} %bitcast.74), kind=kLoop, calls=%fused_computation.42.clone.1 | loop fusion | bytes 23068672 | tf_op jit(solution)/shard_map/while/body/eval_jaxpr/slice | solution.py:24
  344.2 8.2 %copy.26 = bf16[2,1408,1024]{1,2,0:T(8,128)(2,1)} copy(bf16[2,1408,1024]{2,1,0:T(8,128)(2,1)} %get-tuple-element.170) | data formatting | bytes 11534336 | tf_op jit(solution)/shard_map/while/body/eval_jaxpr/slice | solution.py:24
  352.6 3.9 fusion.46
  356.5 2.4 fusion.47
  358.9 1.8 copy-done
  360.7 8.3 %copy.25 = bf16[2,1408,1024]{1,2,0:T(8,128)(2,1)} copy(bf16[2,1408,1024]{2,1,0:T(8,128)(2,1)} %get-tuple-element.169) | data formatting | bytes 11534336 | tf_op jit(solution)/shard_map/while/body/eval_jaxpr/slice | solution.py:25
  369.0 8.8 %divide_convert_fusion.2 = bf16[2,128,8,128]{1,3,2,0:T(8,128)(2,1)S(1)} fusion(bf16[2,1408,8,128]{1,3,2,0:T(8,128)(2,1)} %bitcast.78, f32[2,8,128,1408]{3,2,1,0:T(8,128)} %copy-done, f32[2,8,128]{2,1,0:T(8,128)S(1)} %get-tuple-element.172, pred[2,1408]{1,0:T(4,128)(4,1)S(1)} %broadcast_compare_fusion.2, f32[2,128,8]{1,2,0:T(8,128)S(1)} %bitcast.81), kind=kOutput, calls=%fused_computation.13.clone.1 | convolution fusion | flops 750256128 | bytes 17844992 | tf_op jit(solution)/shard_map/while/body/eval_jaxpr/bhqk,bkhd->bqhd/dot_general | solution.py:38
  378.4 0.8 constant_dynamic-update-slice_fusion.2
  379.2 0.6 dynamic_slice.53
  380.5 1.3 dynamic-slice_bitcast_fusion.4
  381.8 0.7 compare_select_fusion.2
  382.6 10.0 %gather_fusion = bf16[20,128,2048]{2,1,0:T(8,128)(2,1)} fusion(bf16[24,128,2048]{2,1,0:T(8,128)(2,1)} %get-tuple-element.200, s32[1024]{0:T(1024)S(1)} %pad_clamp_fusion.2), kind=kCustom, calls=%fused_computation.clone.1 | custom fusion | bytes 20971600 | tf_op jit(solution)/shard_map/while/body/eval_jaxpr/gather | solution.py:77
  392.6 10.1 %pad_maximum_fusion.3 = bf16[2,11,128,2048]{3,2,1,0:T(8,128)(2,1)} fusion(bf16[2,10,128,2048]{3,2,1,0:T(8,128)(2,1)} %bitcast.76, bf16[2,1,128,2048]{3,2,1,0:T(8,128)(2,1)S(1)} %dynamic-slice_bitcast_fusion.4), kind=kLoop, calls=%fused_computation.1.clone.1 | loop fusion | flops 5767168 | bytes 23068672 | tf_op jit(solution)/shard_map/while/body/eval_jaxpr/concatenate | solution.py:22
  402.7 9.9 %fusion.44 = (bf16[2,1408,1024]{2,1,0:T(8,128)(2,1)}, bf16[2,1408,1024]{2,1,0:T(8,128)(2,1)}) fusion(bf16[2,1408,2048]{2,1,0:T(8,128)(2,1)} %bitcast.74), kind=kLoop, calls=%fused_computation.42.clone.1 | loop fusion | bytes 23068672 | tf_op jit(solution)/shard_map/while/body/eval_jaxpr/slice | solution.py:24
  412.6 8.2 %copy.26 = bf16[2,1408,1024]{1,2,0:T(8,128)(2,1)} copy(bf16[2,1408,1024]{2,1,0:T(8,128)(2,1)} %get-tuple-element.170) | data formatting | bytes 11534336 | tf_op jit(solution)/shard_map/while/body/eval_jaxpr/slice | solution.py:24
  421.1 3.9 fusion.46
  424.9 2.4 fusion.47
  427.4 1.8 copy-done
  429.1 8.3 %copy.25 = bf16[2,1408,1024]{1,2,0:T(8,128)(2,1)} copy(bf16[2,1408,1024]{2,1,0:T(8,128)(2,1)} %get-tuple-element.169) | data formatting | bytes 11534336 | tf_op jit(solution)/shard_map/while/body/eval_jaxpr/slice | solution.py:25
  437.5 8.8 %divide_convert_fusion.2 = bf16[2,128,8,128]{1,3,2,0:T(8,128)(2,1)S(1)} fusion(bf16[2,1408,8,128]{1,3,2,0:T(8,128)(2,1)} %bitcast.78, f32[2,8,128,1408]{3,2,1,0:T(8,128)} %copy-done, f32[2,8,128]{2,1,0:T(8,128)S(1)} %get-tuple-element.172, pred[2,1408]{1,0:T(4,128)(4,1)S(1)} %broadcast_compare_fusion.2, f32[2,128,8]{1,2,0:T(8,128)S(1)} %bitcast.81), kind=kOutput, calls=%fused_computation.13.clone.1 | convolution fusion | flops 750256128 | bytes 17844992 | tf_op jit(solution)/shard_map/while/body/eval_jaxpr/bhqk,bkhd->bqhd/dot_general | solution.py:38
  446.8 0.8 constant_dynamic-update-slice_fusion.2
  447.6 5.9 %convolution_convert_fusion.3 = bf16[1024,1024]{1,0:T(8,128)(2,1)} fusion(bf16[1024,1024]{1,0:T(8,128)(2,1)} %bitcast.83, bf16[1024,1024]{1,0:T(8,128)(2,1)} %all-gather.5.cloned.1.call-done), kind=kOutput, calls=%fused_computation.41 | convolution fusion | flops 2148532224 | bytes 6291456 | tf_op jit(solution)/shard_map/dot_general | solution.py:90
  (55 shorter events, 3.4 us)
Async XLA Ops:
  6.5 120.5 %all-gather.3.cloned.1.call-start = ((), (), s32[]{:S(2)}) async-start(), calls=%async_computation | async-start | bytes 7864320 | tf_op jit(solution)/shard_map/all_gather | solution.py:53
  7.3 440.4 %all-gather.5.cloned.1.call-start = ((), (), s32[]{:S(2)}) async-start(), calls=%async_computation.1 | async-start | bytes 2621440 | tf_op jit(solution)/shard_map/all_gather | solution.py:92
  7.3 132.3 %collective-permute-start.1 = (bf16[1024,1024]{1,0:T(8,128)(2,1)}, bf16[1024,1024]{1,0:T(8,128)(2,1)}, u32[]{:S(2)}, u32[]{:S(2)}) collective-permute-start(bf16[1024,1024]{1,0:T(8,128)(2,1)} %param.7), channel_id=1, source_target_pairs={{0,28},{4,0},{8,4},{12,8},{16,12},{20,16},{24,20},{28,24},{1,29},{... | collective-permute-start | bytes 6291464 | tf_op jit(solution)/shard_map/ppermute | solution.py:15
  10.7 137.1 %collective-permute-start = (bf16[1024,1024]{1,0:T(8,128)(2,1)}, bf16[1024,1024]{1,0:T(8,128)(2,1)S(1)}, u32[]{:S(2)}, u32[]{:S(2)}) collective-permute-start(bf16[1024,1024]{1,0:T(8,128)(2,1)} %param.7), channel_id=1, source_target_pairs={{0,4},{4,8},{8,12},{12,16},{16,20},{20,24},{24,28},{28,0},{1,5},{5... | collective-permute-start | bytes 6291464 | tf_op jit(solution)/shard_map/ppermute | solution.py:15
  136.4 3.2 copy-start.1
  136.4 5.1 %copy-start.2 = (bf16[1024,3072]{1,0:T(8,128)(2,1)S(1)}, bf16[1024,3072]{1,0:T(8,128)(2,1)}, u32[]{:S(2)}) copy-start(bf16[1024,3072]{1,0:T(8,128)(2,1)} %all-gather.3.cloned.1.call-done) | copy-start | bytes 18874372
  147.8 4.8 %slice-start = ((bf16[1024,3072]{1,0:T(8,128)(2,1)}), bf16[1024,2048]{1,0:T(8,128)(2,1)S(1)}, s32[]{:S(2)}) async-start(bf16[1024,3072]{1,0:T(8,128)(2,1)} %copy-done.1), calls=%async_computation.2 | async-start | bytes 8388608 | tf_op jit(solution)/shard_map/slice | solution.py:64
  152.6 21.3 %slice-start.1 = ((bf16[1024,3072]{1,0:T(8,128)(2,1)}), bf16[1024,1024]{1,0:T(8,128)(2,1)S(1)}, s32[]{:S(2)}) async-start(bf16[1024,3072]{1,0:T(8,128)(2,1)} %copy-done.1), calls=%async_computation.3 | async-start | bytes 4194304 | tf_op jit(solution)/shard_map/slice | solution.py:63
  219.6 4.2 copy-start
  288.1 4.2 copy-start
  356.5 4.2 copy-start
  424.9 4.2 copy-start
Sparse Core Ops, SparseCore 0:
  8.9 118.0 all-gather.2
  128.6 43.8 all-gather.4
where the time goes:
time: 463 us; the launch traced here: 460 us
  local copies, waits for them, and re-layouts  173 us (37%)
  waiting for transfers between devices  116 us (25%)
  matrix products  77.1 us (17%)
  other arithmetic  74.4 us (16%)
  between operations  13.5 us (3%)
    all_gather x1, waiting for transfers between devices, shards(): weight_rows = lax.all_gather(w_qkv, 'fsdp', axis=0, tiled=True)  115 us
    slice x8, local copies, waits for them, and re-layouts, attend(): keyvals[..., :feature_width].reshape(block_count, -1, HEADS, head_width)  72.7 us
    concatenate x4, other arithmetic, attend(): keyvals = jnp.concatenate([own_blocks[:, None], picked], axis=1)  40.3 us
    gather x4, local copies, waits for them, and re-layouts, one_group(): picked = pool[layout_part]  40 us
    dot_general x4, matrix products, attend(): jnp.einsum('bhqk,bkhd->bqhd', rounded, value_heads, preferred_element_typ...  35.2 us
    slice x4, local copies, waits for them, and re-layouts, attend(): keyvals[..., feature_width:].reshape(block_count, -1, HEADS, head_width)  33.3 us
    concatenate x1, other arithmetic, shards(): jnp.concatenate([sums[1].astype(jnp.bfloat16), keyvals, sums[2].astype(jn...  21.3 us
    dot_general x4, matrix products, attend(): jnp.einsum('bqhd,bkhd->bhqk', query_heads, key_heads, preferred_element_t...  15.5 us
  transfers between devices with their start and end apart: 4, of which 1 were waited for; matrix products, arithmetic and copies ran while one was open for 67% of the time, Pallas kernels for 0%

commit v1 on v0

--- a/solution.py
+++ b/solution.py
@@ -7,6 +7,28 @@
 HEADS = 8
 BLOCK = 128
 KEY_BLOCKS = 10
+
+
+def in_order(parts, dim):
+    parts = jnp.moveaxis(parts, 0, dim)
+    shape = parts.shape
+    return parts.reshape(*shape[:dim], shape[dim] * shape[dim + 1], *shape[dim + 2 :])
+
+
+def ring_gather(x, axis, dim):
+    length = lax.axis_size(axis)
+    pairs = [(i, (i + 1) % length) for i in range(length)]
+    back = [(b, a) for a, b in pairs]
+    lower, upper = ([], [])
+    for lap in range(length - 1):
+        if lap % 2 == 0:
+            lower.append(lax.ppermute(lower[-1] if lower else x, axis, pairs))
+        else:
+            upper.append(lax.ppermute(upper[-1] if upper else x, axis, back))
+    pieces = jnp.stack([*lower[::-1], x, *upper])
+    shift = lax.axis_index(axis) - len(lower)
+    pieces = pieces[(jnp.arange(length) - shift) % length]
+    return in_order(pieces, dim)
 
 
 def from_behind(value, axis, steps):
@@ -50,7 +72,7 @@
     for member in range(1, len(sources)):
         start_sums.append(jnp.zeros((row_count, 2 * feature_width), jnp.float32))
     start_sums = tuple(start_sums)
-    weight_rows = lax.all_gather(w_qkv, "fsdp", axis=0, tiled=True)
+    weight_rows = ring_gather(w_qkv, "fsdp", 0)
     own_cols = sources[0]
     fresh = [jnp.dot(own_cols, weight_rows, preferred_element_type=jnp.float32)]
     for member in range(1, len(sources)):

time: 463 us -> 503 us (1.086); the launches traced: 460 us -> 495 us
  local copies, waits for them, and re-layouts: 173 us -> 189 us
  waiting for transfers between devices: 116 us -> 125 us
  other arithmetic: 74.4 us -> 79.7 us
    ppermute x0 -> x3, waiting for transfers between devices: none -> 125 us  [the longest x2 93.8 us: ring_gather(): lower.append(lax.ppermute(lower[-1] if lower else x, axis, pairs))]
    all_gather x1 -> x0, waiting for transfers between devices: 115 us -> none  [shards(): weight_rows = lax.all_gather(w_qkv, 'fsdp', axis=0, tiled=True)]
    while x16, local copies, waits for them, and re-layouts: 7.54 us -> 17.2 us
    gather x0 -> x1, local copies, waits for them, and re-layouts: none -> 6.52 us  [ring_gather(): pieces = pieces[(jnp.arange(length) - shift) % length]]
    another operation x0 -> x1, other arithmetic: none -> 5.22 us  [ring_gather(): pieces = jnp.stack([*lower[::-1], x, *upper])]
    ppermute x0 -> x3, starting transfers between devices: none -> 5.08 us  [the longest x2 3.05 us: ring_gather(): lower.append(lax.ppermute(lower[-1] if lower else x, axis, pairs))]
  transfers between devices with their start and end apart: 4 -> 6, of which waited for: 1 -> 3; matrix products, arithmetic and copies ran while one was open for 67% -> 65% of each run, Pallas kernels for 0% -> 0%
where the time goes in v1:
time: 503 us; the launch traced here: 495 us
  local copies, waits for them, and re-layouts  189 us (38%)
  waiting for transfers between devices  125 us (25%)
  other arithmetic  79.7 us (16%)
  matrix products  79 us (16%)
  between operations  13.5 us (3%)
  starting transfers between devices  5.6 us (1%)
    ppermute x2, waiting for transfers between devices, ring_gather(): lower.append(lax.ppermute(lower[-1] if lower else x, axis, pairs))  93.8 us
    slice x8, local copies, waits for them, and re-layouts, attend(): keyvals[..., :feature_width].reshape(block_count, -1, HEADS, head_width)  72.7 us
    concatenate x4, other arithmetic, attend(): keyvals = jnp.concatenate([own_blocks[:, None], picked], axis=1)  40.3 us
    gather x4, local copies, waits for them, and re-layouts, one_group(): picked = pool[layout_part]  40 us
    dot_general x4, matrix products, attend(): jnp.einsum('bhqk,bkhd->bqhd', rounded, value_heads, preferred_element_typ...  35.2 us
    slice x4, local copies, waits for them, and re-layouts, attend(): keyvals[..., feature_width:].reshape(block_count, -1, HEADS, head_width)  33.4 us
    ppermute x1, waiting for transfers between devices, ring_gather(): upper.append(lax.ppermute(upper[-1] if upper else x, axis, back))  31.2 us
    concatenate x1, other arithmetic, shards(): jnp.concatenate([sums[1].astype(jnp.bfloat16), keyvals, sums[2].astype(jn...  21.3 us
  transfers between devices with their start and end apart: 6, of which 3 were waited for; matrix products, arithmetic and copies ran while one was open for 65% of the time, Pallas kernels for 0%

profile of v1, /device:TPU:0, one launch (start us, length us, event | category | flops | bytes accessed | tf_op | source)
XLA Modules:
  0.0 494.5 jit_solution(3664862388874395987)
XLA Ops:
  6.5 3.1 collective-permute-start
  9.6 2.0 collective-permute-start.2
  11.6 35.5 %collective-permute-done = bf16[256,3072]{1,0:T(8,128)(2,1)S(1)} collective-permute-done((bf16[256,3072]{1,0:T(8,128)(2,1)}, bf16[256,3072]{1,0:T(8,128)(2,1)S(1)}, u32[]{:S(2)}, u32[]{:S(2)}) %collective-permute-start) | collective-permute-done | bytes 1572896 | tf_op jit(solution)/shard_map/ppermute | solution.py:25
  47.7 0.7 reshape.196
  48.4 31.2 %collective-permute-done.2 = bf16[256,3072]{1,0:T(8,128)(2,1)S(1)} collective-permute-done((bf16[256,3072]{1,0:T(8,128)(2,1)}, bf16[256,3072]{1,0:T(8,128)(2,1)S(1)}, u32[]{:S(2)}, u32[]{:S(2)}) %collective-permute-start.2) | collective-permute-done | bytes 1572896 | tf_op jit(solution)/shard_map/ppermute | solution.py:27
  79.6 58.3 %collective-permute-done.1 = bf16[256,3072]{1,0:T(8,128)(2,1)} collective-permute-done((bf16[256,3072]{1,0:T(8,128)(2,1)S(1)}, bf16[256,3072]{1,0:T(8,128)(2,1)}, u32[]{:S(2)}, u32[]{:S(2)}) %collective-permute-start.1) | collective-permute-done | bytes 1572896 | tf_op jit(solution)/shard_map/ppermute | solution.py:25
  137.9 5.2 %pad_maximum_fusion.2 = bf16[4,256,3072]{2,1,0:T(8,128)(2,1)} fusion(bf16[1,256,3072]{2,1,0:T(8,128)(2,1)S(1)} %bitcast.99, bf16[1,256,3072]{2,1,0:T(8,128)(2,1)} %bitcast.97, bf16[1,256,3072]{2,1,0:T(8,128)(2,1)S(1)} %bitcast.98, bf16[1,256,3072]{2,1,0:T(8,128)(2,1)} %bitcast.13), kind=kLoop, calls=%fused_computation.37 | loop fusion | flops 9437184 | bytes 12582912 | tf_op jit(solution)/shard_map/stack | solution.py:28
  143.2 6.5 %gather_fusion.1 = bf16[4,256,3072]{2,1,0:T(8,128)(2,1)} fusion(bf16[4,256,3072]{2,1,0:T(8,128)(2,1)} %pad_maximum_fusion.2, s32[1024]{0:T(1024)S(1)} %pad_clamp_fusion.1), kind=kCustom, calls=%fused_computation.1 | custom fusion | bytes 12582928 | tf_op jit(solution)/shard_map/gather | solution.py:30
  149.7 9.6 %convert_bitcast_fusion = bf16[1024,3072]{1,0:T(8,128)(2,1)S(1)} fusion(bf16[1024,1024]{1,0:T(8,128)(2,1)S(1)} %copy-done.3, bf16[1024,3072]{1,0:T(8,128)(2,1)} %bitcast.94), kind=kOutput, calls=%fused_computation.38 | convolution fusion | flops 6445596672 | bytes 14680064 | tf_op jit(solution)/shard_map/dot_general | solution.py:77
  159.4 5.0 %copy-done.2 = bf16[4,256,3072]{2,1,0:T(8,128)(2,1)S(1)} copy-done((bf16[4,256,3072]{2,1,0:T(8,128)(2,1)S(1)}, bf16[4,256,3072]{2,1,0:T(8,128)(2,1)}, u32[]{:S(2)}) %copy-start.2) | copy-done | bytes 6291480
  164.4 6.3 %convert_bitcast_fusion.1 = bf16[1024,2048]{1,0:T(8,128)(2,1)S(1)} fusion(bf16[1024,1024]{1,0:T(8,128)(2,1)} %collective-permute-done.4, bf16[1024,3072]{1,0:T(8,128)(2,1)S(1)} %bitcast.95), kind=kOutput, calls=%fused_computation.39 | convolution fusion | flops 4297064448 | bytes 10485760 | tf_op jit(solution)/shard_map/dot_general | solution.py:81
  170.8 6.5 %convert_bitcast_fusion.2 = bf16[1024,2048]{1,0:T(8,128)(2,1)S(1)} fusion(bf16[1024,1024]{1,0:T(8,128)(2,1)} %collective-permute-done.3, bf16[1024,3072]{1,0:T(8,128)(2,1)S(1)} %bitcast.96), kind=kOutput, calls=%fused_computation.40 | convolution fusion | flops 4297064448 | bytes 10485760 | tf_op jit(solution)/shard_map/dot_general | solution.py:81
  177.3 21.3 %pad_maximum_fusion.1 = bf16[3072,2048]{1,0:T(8,128)(2,1)} fusion(bf16[1024,2048]{1,0:T(8,128)(2,1)S(1)} %convert_bitcast_fusion.1, bf16[1024,2048]{1,0:T(8,128)(2,1)S(1)} %slice-done, bf16[1024,2048]{1,0:T(8,128)(2,1)S(1)} %convert_bitcast_fusion.2), kind=kLoop, calls=%fused_computation.36 | loop fusion | flops 37748736 | bytes 25165824 | tf_op jit(solution)/shard_map/concatenate | solution.py:87
  198.6 283.2 %while.12 = (s32[]{:T(128)}, bf16[4,256,1024]{2,1,0:T(8,128)(2,1)}, s32[4]{0:T(128)S(1)}, bf16[24,128,2048]{2,1,0:T(8,128)(2,1)}, s32[4,2,10]{2,1,0:T(2,128)}, /...) while((s32[]{:T(128)}, bf16[4,256,1024]{2,1,0:T(8,128)(2,1)}, ...), condition=%wide.region_3.4_spmd, body=%wide.region_0.3_spmd.sunk | while | flops 1514416896 | bytes 190909680 | solution.py:102
  198.6 0.6 dynamic_slice.53
  199.8 1.3 dynamic-slice_bitcast_fusion.4
  201.1 0.7 compare_select_fusion.5
  201.9 10.0 %gather_fusion = bf16[20,128,2048]{2,1,0:T(8,128)(2,1)} fusion(bf16[24,128,2048]{2,1,0:T(8,128)(2,1)} %get-tuple-element.200, s32[1024]{0:T(1024)S(1)} %pad_clamp_fusion.3), kind=kCustom, calls=%fused_computation.clone.1 | custom fusion | bytes 20971600 | tf_op jit(solution)/shard_map/while/body/eval_jaxpr/gather | solution.py:99
  211.9 10.1 %pad_maximum_fusion.4 = bf16[2,11,128,2048]{3,2,1,0:T(8,128)(2,1)} fusion(bf16[2,10,128,2048]{3,2,1,0:T(8,128)(2,1)} %bitcast.89, bf16[2,1,128,2048]{3,2,1,0:T(8,128)(2,1)S(1)} %dynamic-slice_bitcast_fusion.4), kind=kLoop, calls=%fused_computation.2.clone.1 | loop fusion | flops 5767168 | bytes 23068672 | tf_op jit(solution)/shard_map/while/body/eval_jaxpr/concatenate | solution.py:44
  222.0 9.9 %fusion.46 = (bf16[2,1408,1024]{2,1,0:T(8,128)(2,1)}, bf16[2,1408,1024]{2,1,0:T(8,128)(2,1)}) fusion(bf16[2,1408,2048]{2,1,0:T(8,128)(2,1)} %bitcast.87), kind=kLoop, calls=%fused_computation.51.clone.1 | loop fusion | bytes 23068672 | tf_op jit(solution)/shard_map/while/body/eval_jaxpr/slice | solution.py:46
  231.9 8.2 %copy.26 = bf16[2,1408,1024]{1,2,0:T(8,128)(2,1)} copy(bf16[2,1408,1024]{2,1,0:T(8,128)(2,1)} %get-tuple-element.170) | data formatting | bytes 11534336 | tf_op jit(solution)/shard_map/while/body/eval_jaxpr/slice | solution.py:46
  240.4 3.9 fusion.48
  244.3 4.2 copy-done
  248.5 2.4 fusion.49
  250.9 8.3 %copy.25 = bf16[2,1408,1024]{1,2,0:T(8,128)(2,1)} copy(bf16[2,1408,1024]{2,1,0:T(8,128)(2,1)} %get-tuple-element.169) | data formatting | bytes 11534336 | tf_op jit(solution)/shard_map/while/body/eval_jaxpr/slice | solution.py:47
  259.2 8.8 %divide_convert_fusion.2 = bf16[2,128,8,128]{1,3,2,0:T(8,128)(2,1)S(1)} fusion(bf16[2,1408,8,128]{1,3,2,0:T(8,128)(2,1)} %bitcast.91, f32[2,8,128,1408]{3,2,1,0:T(8,128)} %copy-done, f32[2,8,128]{2,1,0:T(8,128)S(1)} %get-tuple-element.172, pred[2,1408]{1,0:T(4,128)(4,1)S(1)} %broadcast_compare_fusion.2, f32[2,128,8]{1,2,0:T(8,128)S(1)} %bitcast.100), kind=kOutput, calls=%fused_computation.14.clone.1 | convolution fusion | flops 750256128 | bytes 17844992 | tf_op jit(solution)/shard_map/while/body/eval_jaxpr/bhqk,bkhd->bqhd/dot_general | solution.py:60
  268.6 0.8 constant_dynamic-update-slice_fusion.2
  270.6 1.3 dynamic-slice_bitcast_fusion.4
  271.9 0.7 compare_select_fusion.5
  272.7 10.0 %gather_fusion = bf16[20,128,2048]{2,1,0:T(8,128)(2,1)} fusion(bf16[24,128,2048]{2,1,0:T(8,128)(2,1)} %get-tuple-element.200, s32[1024]{0:T(1024)S(1)} %pad_clamp_fusion.3), kind=kCustom, calls=%fused_computation.clone.1 | custom fusion | bytes 20971600 | tf_op jit(solution)/shard_map/while/body/eval_jaxpr/gather | solution.py:99
  282.7 10.1 %pad_maximum_fusion.4 = bf16[2,11,128,2048]{3,2,1,0:T(8,128)(2,1)} fusion(bf16[2,10,128,2048]{3,2,1,0:T(8,128)(2,1)} %bitcast.89, bf16[2,1,128,2048]{3,2,1,0:T(8,128)(2,1)S(1)} %dynamic-slice_bitcast_fusion.4), kind=kLoop, calls=%fused_computation.2.clone.1 | loop fusion | flops 5767168 | bytes 23068672 | tf_op jit(solution)/shard_map/while/body/eval_jaxpr/concatenate | solution.py:44
  292.8 9.9 %fusion.46 = (bf16[2,1408,1024]{2,1,0:T(8,128)(2,1)}, bf16[2,1408,1024]{2,1,0:T(8,128)(2,1)}) fusion(bf16[2,1408,2048]{2,1,0:T(8,128)(2,1)} %bitcast.87), kind=kLoop, calls=%fused_computation.51.clone.1 | loop fusion | bytes 23068672 | tf_op jit(solution)/shard_map/while/body/eval_jaxpr/slice | solution.py:46
  302.7 8.2 %copy.26 = bf16[2,1408,1024]{1,2,0:T(8,128)(2,1)} copy(bf16[2,1408,1024]{2,1,0:T(8,128)(2,1)} %get-tuple-element.170) | data formatting | bytes 11534336 | tf_op jit(solution)/shard_map/while/body/eval_jaxpr/slice | solution.py:46
  311.2 3.9 fusion.48
  315.1 4.2 copy-done
  319.3 2.4 fusion.49
  321.7 8.3 %copy.25 = bf16[2,1408,1024]{1,2,0:T(8,128)(2,1)} copy(bf16[2,1408,1024]{2,1,0:T(8,128)(2,1)} %get-tuple-element.169) | data formatting | bytes 11534336 | tf_op jit(solution)/shard_map/while/body/eval_jaxpr/slice | solution.py:47
  330.0 8.8 %divide_convert_fusion.2 = bf16[2,128,8,128]{1,3,2,0:T(8,128)(2,1)S(1)} fusion(bf16[2,1408,8,128]{1,3,2,0:T(8,128)(2,1)} %bitcast.91, f32[2,8,128,1408]{3,2,1,0:T(8,128)} %copy-done, f32[2,8,128]{2,1,0:T(8,128)S(1)} %get-tuple-element.172, pred[2,1408]{1,0:T(4,128)(4,1)S(1)} %broadcast_compare_fusion.2, f32[2,128,8]{1,2,0:T(8,128)S(1)} %bitcast.100), kind=kOutput, calls=%fused_computation.14.clone.1 | convolution fusion | flops 750256128 | bytes 17844992 | tf_op jit(solution)/shard_map/while/body/eval_jaxpr/bhqk,bkhd->bqhd/dot_general | solution.py:60
  339.4 0.9 constant_dynamic-update-slice_fusion.2
  341.5 1.3 dynamic-slice_bitcast_fusion.4
  342.8 0.7 compare_select_fusion.5
  343.5 10.0 %gather_fusion = bf16[20,128,2048]{2,1,0:T(8,128)(2,1)} fusion(bf16[24,128,2048]{2,1,0:T(8,128)(2,1)} %get-tuple-element.200, s32[1024]{0:T(1024)S(1)} %pad_clamp_fusion.3), kind=kCustom, calls=%fused_computation.clone.1 | custom fusion | bytes 20971600 | tf_op jit(solution)/shard_map/while/body/eval_jaxpr/gather | solution.py:99
  353.5 10.1 %pad_maximum_fusion.4 = bf16[2,11,128,2048]{3,2,1,0:T(8,128)(2,1)} fusion(bf16[2,10,128,2048]{3,2,1,0:T(8,128)(2,1)} %bitcast.89, bf16[2,1,128,2048]{3,2,1,0:T(8,128)(2,1)S(1)} %dynamic-slice_bitcast_fusion.4), kind=kLoop, calls=%fused_computation.2.clone.1 | loop fusion | flops 5767168 | bytes 23068672 | tf_op jit(solution)/shard_map/while/body/eval_jaxpr/concatenate | solution.py:44
  363.6 9.9 %fusion.46 = (bf16[2,1408,1024]{2,1,0:T(8,128)(2,1)}, bf16[2,1408,1024]{2,1,0:T(8,128)(2,1)}) fusion(bf16[2,1408,2048]{2,1,0:T(8,128)(2,1)} %bitcast.87), kind=kLoop, calls=%fused_computation.51.clone.1 | loop fusion | bytes 23068672 | tf_op jit(solution)/shard_map/while/body/eval_jaxpr/slice | solution.py:46
  373.6 8.2 %copy.26 = bf16[2,1408,1024]{1,2,0:T(8,128)(2,1)} copy(bf16[2,1408,1024]{2,1,0:T(8,128)(2,1)} %get-tuple-element.170) | data formatting | bytes 11534336 | tf_op jit(solution)/shard_map/while/body/eval_jaxpr/slice | solution.py:46
  382.0 3.9 fusion.48
  385.9 4.2 copy-done
  390.1 2.4 fusion.49
  392.5 8.3 %copy.25 = bf16[2,1408,1024]{1,2,0:T(8,128)(2,1)} copy(bf16[2,1408,1024]{2,1,0:T(8,128)(2,1)} %get-tuple-element.169) | data formatting | bytes 11534336 | tf_op jit(solution)/shard_map/while/body/eval_jaxpr/slice | solution.py:47
  400.9 8.8 %divide_convert_fusion.2 = bf16[2,128,8,128]{1,3,2,0:T(8,128)(2,1)S(1)} fusion(bf16[2,1408,8,128]{1,3,2,0:T(8,128)(2,1)} %bitcast.91, f32[2,8,128,1408]{3,2,1,0:T(8,128)} %copy-done, f32[2,8,128]{2,1,0:T(8,128)S(1)} %get-tuple-element.172, pred[2,1408]{1,0:T(4,128)(4,1)S(1)} %broadcast_compare_fusion.2, f32[2,128,8]{1,2,0:T(8,128)S(1)} %bitcast.100), kind=kOutput, calls=%fused_computation.14.clone.1 | convolution fusion | flops 750256128 | bytes 17844992 | tf_op jit(solution)/shard_map/while/body/eval_jaxpr/bhqk,bkhd->bqhd/dot_general | solution.py:60
  410.2 0.8 constant_dynamic-update-slice_fusion.2
  412.2 1.3 dynamic-slice_bitcast_fusion.4
  413.5 0.7 compare_select_fusion.5
  414.3 10.0 %gather_fusion = bf16[20,128,2048]{2,1,0:T(8,128)(2,1)} fusion(bf16[24,128,2048]{2,1,0:T(8,128)(2,1)} %get-tuple-element.200, s32[1024]{0:T(1024)S(1)} %pad_clamp_fusion.3), kind=kCustom, calls=%fused_computation.clone.1 | custom fusion | bytes 20971600 | tf_op jit(solution)/shard_map/while/body/eval_jaxpr/gather | solution.py:99
  424.3 10.1 %pad_maximum_fusion.4 = bf16[2,11,128,2048]{3,2,1,0:T(8,128)(2,1)} fusion(bf16[2,10,128,2048]{3,2,1,0:T(8,128)(2,1)} %bitcast.89, bf16[2,1,128,2048]{3,2,1,0:T(8,128)(2,1)S(1)} %dynamic-slice_bitcast_fusion.4), kind=kLoop, calls=%fused_computation.2.clone.1 | loop fusion | flops 5767168 | bytes 23068672 | tf_op jit(solution)/shard_map/while/body/eval_jaxpr/concatenate | solution.py:44
  434.4 9.9 %fusion.46 = (bf16[2,1408,1024]{2,1,0:T(8,128)(2,1)}, bf16[2,1408,1024]{2,1,0:T(8,128)(2,1)}) fusion(bf16[2,1408,2048]{2,1,0:T(8,128)(2,1)} %bitcast.87), kind=kLoop, calls=%fused_computation.51.clone.1 | loop fusion | bytes 23068672 | tf_op jit(solution)/shard_map/while/body/eval_jaxpr/slice | solution.py:46
  444.4 8.2 %copy.26 = bf16[2,1408,1024]{1,2,0:T(8,128)(2,1)} copy(bf16[2,1408,1024]{2,1,0:T(8,128)(2,1)} %get-tuple-element.170) | data formatting | bytes 11534336 | tf_op jit(solution)/shard_map/while/body/eval_jaxpr/slice | solution.py:46
  452.8 3.9 fusion.48
  456.7 4.2 copy-done
  460.9 2.4 fusion.49
  463.3 8.3 %copy.25 = bf16[2,1408,1024]{1,2,0:T(8,128)(2,1)} copy(bf16[2,1408,1024]{2,1,0:T(8,128)(2,1)} %get-tuple-element.169) | data formatting | bytes 11534336 | tf_op jit(solution)/shard_map/while/body/eval_jaxpr/slice | solution.py:47
  471.6 8.8 %divide_convert_fusion.2 = bf16[2,128,8,128]{1,3,2,0:T(8,128)(2,1)S(1)} fusion(bf16[2,1408,8,128]{1,3,2,0:T(8,128)(2,1)} %bitcast.91, f32[2,8,128,1408]{3,2,1,0:T(8,128)} %copy-done, f32[2,8,128]{2,1,0:T(8,128)S(1)} %get-tuple-element.172, pred[2,1408]{1,0:T(4,128)(4,1)S(1)} %broadcast_compare_fusion.2, f32[2,128,8]{1,2,0:T(8,128)S(1)} %bitcast.100), kind=kOutput, calls=%fused_computation.14.clone.1 | convolution fusion | flops 750256128 | bytes 17844992 | tf_op jit(solution)/shard_map/while/body/eval_jaxpr/bhqk,bkhd->bqhd/dot_general | solution.py:60
  481.0 0.8 constant_dynamic-update-slice_fusion.2
  481.8 5.9 %convolution_convert_fusion = bf16[1024,1024]{1,0:T(8,128)(2,1)} fusion(bf16[1024,1024]{1,0:T(8,128)(2,1)} %bitcast.102, bf16[1024,1024]{1,0:T(8,128)(2,1)} %all-gather.2.cloned.1.call-done), kind=kOutput, calls=%fused_computation.43 | convolution fusion | flops 2148532224 | bytes 6291456 | tf_op jit(solution)/shard_map/dot_general | solution.py:112
  (64 shorter events, 5.7 us)
Async XLA Ops:
  6.5 475.3 %all-gather.2.cloned.1.call-start = ((), (), s32[]{:S(2)}) async-start(), calls=%async_computation | async-start | bytes 2621440 | tf_op jit(solution)/shard_map/all_gather | solution.py:114
  6.5 40.6 %collective-permute-start = (bf16[256,3072]{1,0:T(8,128)(2,1)}, bf16[256,3072]{1,0:T(8,128)(2,1)S(1)}, u32[]{:S(2)}, u32[]{:S(2)}) collective-permute-start(bf16[256,3072]{1,0:T(8,128)(2,1)} %param.8), channel_id=1, source_target_pairs={{0,1},{1,2},{2,3},{3,0},{4,5},{5,6},{6,7},{7,4},{8,9},{9,10},{10,1... | collective-permute-start | bytes 4718600 | tf_op jit(solution)/shard_map/ppermute | solution.py:25
  9.6 70.0 %collective-permute-start.2 = (bf16[256,3072]{1,0:T(8,128)(2,1)}, bf16[256,3072]{1,0:T(8,128)(2,1)S(1)}, u32[]{:S(2)}, u32[]{:S(2)}) collective-permute-start(bf16[256,3072]{1,0:T(8,128)(2,1)} %param.8), channel_id=1, source_target_pairs={{1,0},{2,1},{3,2},{0,3},{5,4},{6,5},{7,6},{4,7},{9,8},{10,9},{11,1... | collective-permute-start | bytes 4718600 | tf_op jit(solution)/shard_map/ppermute | solution.py:27
  47.1 90.8 %collective-permute-start.1 = (bf16[256,3072]{1,0:T(8,128)(2,1)S(1)}, bf16[256,3072]{1,0:T(8,128)(2,1)}, u32[]{:S(2)}, u32[]{:S(2)}) collective-permute-start(bf16[256,3072]{1,0:T(8,128)(2,1)S(1)} %collective-permute-done), channel_id=1, source_target_pairs={{0,1},{1,2},{2,3},{3,0},{4,5},{5,6},{6,7},{7,4},{8,9},{9,10},{10,1... | collective-permute-start | bytes 4718600 | tf_op jit(solution)/shard_map/ppermute | solution.py:25
  47.1 112.2 %collective-permute-start.4 = (bf16[1024,1024]{1,0:T(8,128)(2,1)}, bf16[1024,1024]{1,0:T(8,128)(2,1)}, u32[]{:S(2)}, u32[]{:S(2)}) collective-permute-start(bf16[1024,1024]{1,0:T(8,128)(2,1)} %param.7), channel_id=1, source_target_pairs={{0,28},{4,0},{8,4},{12,8},{16,12},{20,16},{24,20},{28,24},{1,29},{... | collective-permute-start | bytes 6291464 | tf_op jit(solution)/shard_map/ppermute | solution.py:37
  47.4 123.4 %collective-permute-start.3 = (bf16[1024,1024]{1,0:T(8,128)(2,1)}, bf16[1024,1024]{1,0:T(8,128)(2,1)}, u32[]{:S(2)}, u32[]{:S(2)}) collective-permute-start(bf16[1024,1024]{1,0:T(8,128)(2,1)} %param.7), channel_id=1, source_target_pairs={{0,4},{4,8},{8,12},{12,16},{16,20},{20,24},{24,28},{28,0},{1,5},{5... | collective-permute-start | bytes 6291464 | tf_op jit(solution)/shard_map/ppermute | solution.py:37
  143.2 6.5 %copy-start.3 = (bf16[1024,1024]{1,0:T(8,128)(2,1)S(1)}, bf16[1024,1024]{1,0:T(8,128)(2,1)}, u32[]{:S(2)}) copy-start(bf16[1024,1024]{1,0:T(8,128)(2,1)} %param.7) | copy-start | bytes 6291460
  159.3 11.4 %copy-start.1 = (bf16[1024,3072]{1,0:T(8,128)(2,1)}, bf16[1024,3072]{1,0:T(8,128)(2,1)S(1)}, u32[]{:S(2)}) copy-start(bf16[1024,3072]{1,0:T(8,128)(2,1)S(1)} %convert_bitcast_fusion) | copy-start | bytes 18874372
  159.3 5.1 %copy-start.2 = (bf16[4,256,3072]{2,1,0:T(8,128)(2,1)S(1)}, bf16[4,256,3072]{2,1,0:T(8,128)(2,1)}, u32[]{:S(2)}) copy-start(bf16[4,256,3072]{2,1,0:T(8,128)(2,1)} %gather_fusion.1) | copy-start | bytes 18874372
  170.7 6.5 %slice-start = ((bf16[1024,3072]{1,0:T(8,128)(2,1)}), bf16[1024,2048]{1,0:T(8,128)(2,1)S(1)}, s32[]{:S(2)}) async-start(bf16[1024,3072]{1,0:T(8,128)(2,1)} %copy-done.1), calls=%async_computation.1 | async-start | bytes 8388608 | tf_op jit(solution)/shard_map/slice | solution.py:86
  177.3 21.4 %slice-start.1 = ((bf16[1024,3072]{1,0:T(8,128)(2,1)}), bf16[1024,1024]{1,0:T(8,128)(2,1)S(1)}, s32[]{:S(2)}) async-start(bf16[1024,3072]{1,0:T(8,128)(2,1)} %copy-done.1), calls=%async_computation.2 | async-start | bytes 4194304 | tf_op jit(solution)/shard_map/slice | solution.py:85
  244.3 4.2 copy-start
  315.1 4.2 copy-start
  385.9 4.2 copy-start
  456.7 4.2 copy-start
Sparse Core Ops, SparseCore 0:
  47.8 100.0 all-gather.1
